TPU v7x, 32 devices: a whole 2x2x4 slice. The times are simulated.
32 devices in a mesh: gx: 2 (over y), gy: 4 (over x, core), gz: 4 (over z).
Axes of the slice: x: 2, y: 2, z: 4, core: 2. Of those that a mesh axis runs over, the one named last changes fastest.
Arguments:
- fluid_state: float32 [4, 32, 64, 512], P(None, 'gx', 'gy', 'gz'), may hold values from -6 to 6
- shell_disp: float32 [3, 32768], P(None, ('gy', 'gz')), may hold values from -6 to 6
- quad_weights: float32 [32, 32, 64], P(('gx', 'gy', 'gz')), may hold values from 0.25 to 1
- quad_elements: int32 [32, 32, 64], P(('gx', 'gy', 'gz')), may hold values from 0 to 32767
- owner_cells: int32 [32, 32, 64], P(('gx', 'gy', 'gz')), may hold values from 0 to 32767
- owner_counts: int32 [32, 32], P(('gx', 'gy', 'gz')), may hold values from 0 to 64, as said below
Outputs:
- fluid_out: float32 [4, 32, 64, 512], P(None, 'gx', 'gy', 'gz')
- shell_out: float32 [3, 32768], P(None, ('gy', 'gz'))
Inputs may be any that keep to these rules, and one draw needn't show every extreme that they name: `owner_counts`: some owner has 64 live records from every sender; some owner has none from some sender.
All inputs are finite; a program needn't handle non-finite values.
Results may differ from a plain program's by a relative error of at most 0.000023.
Values sent between devices are 32-bit elements; how exact they have to be, the bound alone decides.
A program may use at most 128 MiB of HBM per device.

v0:
```python
import jax
import jax.numpy as jnp
from jax import lax
from jax.sharding import PartitionSpec as P

ITERS = 2
advection = 0.2
penalty = 0.5
relaxation = 0.05


def with_halo(cells, sides, width):
    for axis, dim in sides:
        count = lax.axis_size(axis)
        ends = count - 1
        head = lax.slice_in_dim(cells, 0, width, axis=dim)
        tail = lax.slice_in_dim(cells, cells.shape[dim] - width, cells.shape[dim], axis=dim)
        cells = jnp.concatenate(
            [
                lax.ppermute(tail, axis, [(i, (i + 1) % count) for i in range(ends)]),
                cells,
                lax.ppermute(head, axis, [((i + 1) % count, i) for i in range(ends)]),
            ],
            axis=dim,
        )
    return cells


def smooth_axis(values, axis):
    length = values.shape[axis] - 2
    lower = lax.slice_in_dim(values, 0, length, axis=axis)
    middle = lax.slice_in_dim(values, 1, length + 1, axis=axis)
    upper = lax.slice_in_dim(values, 2, length + 2, axis=axis)
    return 0.25 * lower + 0.5 * middle + 0.25 * upper


def sweep_fluid(padded):
    smoothed = smooth_axis(smooth_axis(smooth_axis(padded, 1), 2), 3)
    center = padded[:, 1:-1, 1:-1, 1:-1]
    grad_x = 0.5 * (padded[:, 2:, 1:-1, 1:-1] - padded[:, :-2, 1:-1, 1:-1])
    grad_y = 0.5 * (padded[:, 1:-1, 2:, 1:-1] - padded[:, 1:-1, :-2, 1:-1])
    grad_z = 0.5 * (padded[:, 1:-1, 1:-1, 2:] - padded[:, 1:-1, 1:-1, :-2])
    convect = center[0:1] * grad_x + center[1:2] * grad_y + center[2:3] * grad_z
    updated = smoothed - advection * convect
    pressure_grad = jnp.stack([grad_x[3], grad_y[3], grad_z[3]])
    return jnp.concatenate([updated[0:3] - advection * pressure_grad, updated[3:4]], 0)


def on_device(fluid_state, shell_disp, quad_weights, quad_elements, owner_cells, owner_counts):
    slots = quad_weights.shape[2]
    elements = quad_elements[0]
    cells_local = owner_cells[0]
    slot_index = jnp.arange(slots, dtype=jnp.int32)[None, :]
    live_mask = (slot_index < owner_counts[0][:, None]).astype(jnp.float32)
    block_shape = fluid_state.shape
    for iteration in range(ITERS):
        padded = with_halo(fluid_state, (("gx", 1), ("gy", 2), ("gz", 3)), 1)
        halfway = sweep_fluid(padded)
        all_nodes = lax.all_gather(shell_disp, ("gy", "gz"), axis=1, tiled=True)
        shell_vel = all_nodes[:, elements]
        records = jnp.concatenate([shell_vel, quad_weights[0][None]], 0)
        received = lax.all_to_all(
            records, ("gx", "gy", "gz"), split_axis=1, concat_axis=1, tiled=True
        )
        flat_vel = halfway[0:3].reshape(3, -1)
        velocity = flat_vel[:, cells_local]
        traction = penalty * received[3][None] * (velocity - received[0:3]) * live_mask[None]
        forcing = jnp.zeros_like(flat_vel).at[:, cells_local].add(traction)
        forcing = forcing.reshape(3, block_shape[1], block_shape[2], block_shape[3])
        fluid_state = jnp.concatenate([halfway[0:3] - forcing, halfway[3:4]], 0)
        returned = lax.all_to_all(
            traction, ("gx", "gy", "gz"), split_axis=1, concat_axis=1, tiled=True
        )
        node_terms = jnp.zeros((3, all_nodes.shape[1]), jnp.float32).at[:, elements].add(returned)
        partial_loads = lax.psum_scatter(node_terms, ("gy", "gz"), scatter_dimension=1, tiled=True)
        node_loads = lax.psum(partial_loads, "gx")
        shell_disp = shell_disp + relaxation * node_loads
    return (fluid_state, shell_disp)


def solution(mesh):
    return jax.shard_map(
        on_device,
        mesh=mesh,
        in_specs=(
            P(None, "gx", "gy", "gz"),
            P(None, ("gy", "gz")),
            P(("gx", "gy", "gz"), None, None),
            P(("gx", "gy", "gz"), None, None),
            P(("gx", "gy", "gz"), None, None),
            P(("gx", "gy", "gz"), None),
        ),
        out_specs=(P(None, "gx", "gy", "gz"), P(None, ("gy", "gz"))),
        check_vma=False,
    )
```

profile of v0, /device:TPU:0, one launch (start us, length us, event | category | flops | bytes accessed | tf_op | source)
XLA Modules:
  0.0 1414.3 jit_solution(13298228462873777052)
XLA Ops:
  7.2 0.8 fusion.46
  8.0 4.9 collective-permute-start
  12.8 1.3 collective-permute-start.1
  15.0 1.1 copy.153
  16.1 359.1 %all_gather.6 = f32[3,32768]{0,1:T(8,128)} all-gather(f32[3,2048]{0,1:T(8,128)S(1)} %copy.153), channel_id=1, replica_groups=mesh['gx'=2,'gy'=4,'gz'=4] {'gy','gz'}, dimensions={1}, use_global_device_ids=true | all-gather | bytes 417792 | tf_op jit(solution)/shard_map/all_gather | solution.py:59
  375.3 11.2 gather_fusion
  387.7 5.4 all-to-all-start
  394.7 2.2 collective-permute-start.2
  396.9 1.3 collective-permute-start.3
  398.2 4.2 copy.142
  403.8 4.3 copy.141
  408.1 4.3 copy.143
  412.5 8.1 pad_maximum_fusion
  420.6 2.6 copy-done.1
  423.9 4.2 collective-permute-start.4
  428.0 1.7 collective-permute-start.5
  429.8 4.6 copy.145
  435.6 1.3 copy.144
  437.0 2.3 copy.146
  439.3 1.9 pad_maximum_fusion.2
  442.6 0.9 fusion.26
  444.3 8.7 copy.157
  453.0 13.3 gather_fusion.1
  466.3 1.6 copy.158
  468.0 1.4 copy.190
  469.4 18.6 %scatter_custom_fusion = f32[3,32768]{0,1:T(8,128)} fusion(s32[2048]{0:T(1024)} %copy-done.35, f32[2048,3]{1,0:T(8,128)} %bitcast.86, f32[]{:T(128)} %constant.10.clone.1), kind=kCustom, calls=%fused_computation.14 | custom fusion | flops 6144 | bytes 393728 | tf_op jit(solution)/shard_map/scatter-add | solution.py:68
  488.0 10.0 copy.161
  498.1 3.4 collective-permute-start.6
  501.5 1.3 collective-permute-start.7
  503.5 10.1 all-to-all-start.1
  514.5 2.2 collective-permute-start.8
  516.6 1.5 collective-permute-start.9
  518.2 4.3 copy.165
  522.5 0.8 reduce.1
  523.4 4.3 copy.164
  527.6 4.2 copy.166
  531.8 8.1 pad_maximum_fusion.1
  540.0 2.6 copy-done
  542.6 3.5 collective-permute-start.10
  546.2 1.3 collective-permute-start.11
  547.5 1.4 copy.191
  548.9 18.6 %scatter_custom_fusion.1 = f32[3,32768]{0,1:T(8,128)} fusion(s32[2048]{0:T(1024)} %copy-done.34, f32[2048,3]{1,0:T(8,128)} %bitcast.87, f32[]{:T(128)} %constant.10.clone.1), kind=kCustom, calls=%fused_computation.12 | custom fusion | flops 6144 | bytes 393728 | tf_op jit(solution)/shard_map/scatter-add | solution.py:74
  567.5 4.6 copy.168
  572.8 1.5 copy.167
  574.2 1.5 copy.169
  575.7 2.2 pad_maximum_fusion.3
  579.3 1.6 fusion.20
  581.1 168.3 %reduce-scatter.3.cloned.1.call-done = f32[3,2048]{0,1:T(8,128)} async-done(((f32[3,32768]{0,1:T(8,128)}), f32[3,2048]{0,1:T(8,128)}) %reduce-scatter.3.cloned.1.call-update) | async-done | bytes 24592 | tf_op jit(solution)/shard_map/reduce_scatter | solution.py:75
  749.3 28.5 %psum.14 = f32[3,2048]{0,1:T(8,128)S(1)} all-reduce(f32[3,2048]{0,1:T(8,128)} %reduce-scatter.3.cloned.1.call-done), channel_id=1, replica_groups=mesh['gx'=2,'gy'=4,'gz'=4] {'gx'}, use_global_device_ids=true, to_apply=%region_3.0 | all-reduce | flops 6144 | bytes 49152 | tf_op jit(solution)/shard_map/psum | solution.py:76
  777.9 353.5 %all_gather.7 = f32[3,32768]{0,1:T(8,128)} all-gather(f32[3,2048]{0,1:T(8,128)S(1)} %multiply_add_fusion.1), channel_id=1, replica_groups=mesh['gx'=2,'gy'=4,'gz'=4] {'gy','gz'}, dimensions={1}, use_global_device_ids=true | all-gather | bytes 417792 | tf_op jit(solution)/shard_map/all_gather | solution.py:59
  1131.4 11.2 gather_fusion.2
  1143.8 5.2 all-to-all-start.2
  1149.1 8.7 copy.182
  1157.8 11.2 gather_fusion.3
  1169.4 0.8 reduce.2
  1171.1 5.8 all-to-all-start.3
  1177.0 7.2 all-to-all-done.3
  1185.5 18.4 %scatter_custom_fusion.3 = f32[3,32768]{0,1:T(8,128)} fusion(s32[2048]{0:T(1024)} %copy-done.34, f32[2048,3]{1,0:T(8,128)S(1)} %bitcast.85, f32[]{:T(128)} %constant.10.clone.1), kind=kCustom, calls=%fused_computation.8 | custom fusion | flops 6144 | bytes 393728 | tf_op jit(solution)/shard_map/scatter-add | solution.py:74
  1204.3 21.6 %scatter_custom_fusion.2 = f32[3,32768]{0,1:T(8,128)} fusion(s32[2048]{0:T(1024)} %copy-done.35, f32[2048,3]{1,0:T(8,128)S(1)} %bitcast.84, f32[]{:T(128)} %constant.10.clone.1), kind=kCustom, calls=%fused_computation.10 | custom fusion | flops 6144 | bytes 393728 | tf_op jit(solution)/shard_map/scatter-add | solution.py:68
  1225.9 10.3 copy.186
  1236.3 0.8 pad_maximum_fusion.25
  1237.2 140.6 %reduce-scatter.5.cloned.1.call-done = f32[3,2048]{0,1:T(8,128)} async-done(((f32[3,32768]{0,1:T(8,128)}), f32[3,2048]{0,1:T(8,128)}) %reduce-scatter.5.cloned.1.call-update) | async-done | bytes 24592 | tf_op jit(solution)/shard_map/reduce_scatter | solution.py:75
  1377.7 28.5 %psum.15 = f32[3,2048]{0,1:T(8,128)S(1)} all-reduce(f32[3,2048]{0,1:T(8,128)} %reduce-scatter.5.cloned.1.call-done), channel_id=1, replica_groups=mesh['gx'=2,'gy'=4,'gz'=4] {'gx'}, use_global_device_ids=true, to_apply=%region_7.0 | all-reduce | flops 6144 | bytes 49152 | tf_op jit(solution)/shard_map/psum | solution.py:76
  1406.3 0.9 copy.189
  (164 shorter events, 17.6 us)
Async XLA Ops:
  8.0 386.0 %collective-permute-start = (f32[4,1,16,128]{3,2,1,0:T(8,128)S(1)}, f32[4,1,16,128]{3,2,1,0:T(8,128)S(1)}, u32[]{:S(2)}, u32[]{:S(2)}) collective-permute-start(f32[4,1,16,128]{3,2,1,0:T(8,128)S(1)} %get-tuple-element.36), channel_id=1, source_target_pairs={{0,16},{1,17},{2,18},{3,19},{4,20},{5,21},{6,22},{7,23},{8,24},{9,... | collective-permute-start | bytes 98312 | tf_op jit(solution)/shard_map/ppermute | solution.py:20
  12.8 381.2 %collective-permute-start.1 = (f32[4,1,16,128]{3,2,1,0:T(8,128)S(1)}, f32[4,1,16,128]{3,2,1,0:T(8,128)S(1)}, u32[]{:S(2)}, u32[]{:S(2)}) collective-permute-start(f32[4,1,16,128]{3,2,1,0:T(8,128)S(1)} %get-tuple-element.35), channel_id=1, source_target_pairs={{16,0},{17,1},{18,2},{19,3},{20,4},{21,5},{22,6},{23,7},{24,8},{25... | collective-permute-start | bytes 98312 | tf_op jit(solution)/shard_map/ppermute | solution.py:22
  14.9 360.3 %copy-start.34 = (s32[2048]{0:T(1024)}, s32[2048]{0:T(1024)S(1)}, u32[]{:S(2)}) copy-start(s32[2048]{0:T(1024)S(1)} %reshape.111) | copy-start | bytes 24580
  15.0 360.3 %copy-start.15 = (s32[2048]{0:T(1024)}, s32[2048]{0:T(1024)S(1)}, u32[]{:S(2)}) copy-start(s32[2048]{0:T(1024)S(1)} %broadcast_clamp_fusion.1) | copy-start | bytes 24580
  16.1 370.8 %copy-start.32 = (f32[1,32,64]{2,1,0:T(8,128)S(1)}, f32[1,32,64]{2,1,0:T(8,128)}, u32[]{:S(2)}) copy-start(f32[1,32,64]{2,1,0:T(8,128)} %param.8) | copy-start | bytes 24580
  16.1 377.0 %copy-start.5 = (f32[4,16,16,128]{3,2,1,0:T(8,128)S(1)}, f32[4,16,16,128]{3,2,1,0:T(8,128)}, u32[]{:S(2)}) copy-start(f32[4,16,16,128]{3,2,1,0:T(8,128)} %param.6) | copy-start | bytes 1572868
  16.1 377.7 %copy-start.36 = (s32[1,32,64]{2,1,0:T(8,128)S(1)}, s32[1,32,64]{2,1,0:T(8,128)}, u32[]{:S(2)}) copy-start(s32[1,32,64]{2,1,0:T(8,128)} %param.10) | copy-start | bytes 24580
  16.1 377.7 %copy-start.37 = (s32[1,32]{1,0:T(1,128)S(1)}, s32[1,32]{1,0:T(1,128)}, u32[]{:S(2)}) copy-start(s32[1,32]{1,0:T(1,128)} %param.11) | copy-start | bytes 388
  387.7 14.7 %all-to-all-start = ((f32[32,1,256]{2,1,0:T(1,128)}), f32[32,1,256]{2,1,0:T(1,128)S(1)}, u32[]{:S(2)}, u32[]{:S(2)}) async-start(f32[32,1,256]{2,1,0:T(1,128)} %reshape.189), calls=%async_computation | async-start | bytes 65536 | tf_op jit(solution)/shard_map/all_to_all | solution.py:62
  393.9 8.4 copy-start.35
  393.9 2.9 copy-start.28
  394.0 0.6 copy-start.30
  394.6 13.5 copy-start.9
  394.7 9.2 collective-permute-start.2
  396.9 11.2 collective-permute-start.3
  398.2 54.8 %copy-start.17 = (s32[2048]{0:T(1024)}, s32[2048]{0:T(1024)S(1)}, u32[]{:S(2)}) copy-start(s32[2048]{0:T(1024)S(1)} %broadcast_clamp_fusion) | copy-start | bytes 24580
  403.8 8.7 copy-start.11
  420.6 2.6 copy-start.1
  423.9 11.8 collective-permute-start.4
  428.0 9.0 collective-permute-start.5
  441.2 1.2 copy-start.2
  441.2 1.3 copy-start.10
  441.2 1.3 copy-start.13
  441.2 1.4 copy-start.14
  441.2 1.3 copy-start.21
  441.2 1.3 copy-start.23
  441.2 1.3 copy-start.29
  441.3 1.3 copy-start.31
  443.4 0.8 copy-start.7
  444.3 23.6 %copy-start.12 = (f32[32,4,64]{2,1,0:T(4,128)S(1)}, f32[32,4,64]{2,1,0:T(4,128)}, u32[]{:S(2)}) copy-start(f32[32,4,64]{2,1,0:T(4,128)} %copy-done.11) | copy-start | bytes 98308
  488.0 10.0 copy-start.8
  498.1 15.6 %collective-permute-start.6 = (f32[4,1,16,128]{3,2,1,0:T(8,128)S(1)}, f32[4,1,16,128]{3,2,1,0:T(8,128)S(1)}, u32[]{:S(2)}, u32[]{:S(2)}) collective-permute-start(f32[4,1,16,128]{3,2,1,0:T(8,128)S(1)} %get-tuple-element.30), channel_id=1, source_target_pairs={{0,16},{1,17},{2,18},{3,19},{4,20},{5,21},{6,22},{7,23},{8,24},{9,... | collective-permute-start | bytes 98312 | tf_op jit(solution)/shard_map/ppermute | solution.py:20
  501.5 12.3 collective-permute-start.7
  503.5 19.0 %all-to-all-start.1 = ((f32[32,1,192]{2,1,0:T(1,128)}), f32[32,1,192]{2,1,0:T(1,128)S(1)}, u32[]{:S(2)}, u32[]{:S(2)}) async-start(f32[32,1,192]{2,1,0:T(1,128)} %reshape.191), calls=%async_computation.1 | async-start | bytes 65536 | tf_op jit(solution)/shard_map/all_to_all | solution.py:71
  513.7 235.7 %reduce-scatter.3.cloned.1.call-start = ((), (), s32[]{:S(2)}) async-start(), calls=%async_computation.6 | async-start | bytes 17825792 | tf_op jit(solution)/shard_map/reduce_scatter | solution.py:75
  513.7 13.9 copy-start.24
  513.7 0.6 copy-start.26
  514.5 8.9 collective-permute-start.8
  516.6 11.0 collective-permute-start.9
  527.6 12.3 copy-start.19
  540.0 2.6 copy-start
  542.6 30.2 %collective-permute-start.10 = (f32[4,18,18,1]{2,1,3,0:T(8,128)S(1)}, f32[4,18,18,1]{2,1,3,0:T(8,128)S(1)}, u32[]{:S(2)}, u32[]{:S(2)}) collective-permute-start(f32[4,18,18,1]{2,1,3,0:T(8,128)S(1)} %get-tuple-element.22), channel_id=1, source_target_pairs={{0,1},{1,2},{2,3},{4,5},{5,6},{6,7},{8,9},{9,10},{10,11},{12,13},{... | collective-permute-start | bytes 15560 | tf_op jit(solution)/shard_map/ppermute | solution.py:20
  546.2 28.1 %collective-permute-start.11 = (f32[4,18,18,1]{2,1,3,0:T(8,128)S(1)}, f32[4,18,18,1]{2,1,3,0:T(8,128)S(1)}, u32[]{:S(2)}, u32[]{:S(2)}) collective-permute-start(f32[4,18,18,1]{2,1,3,0:T(8,128)S(1)} %get-tuple-element.23), channel_id=1, source_target_pairs={{1,0},{2,1},{3,2},{5,4},{6,5},{7,6},{9,8},{10,9},{11,10},{13,12},{... | collective-permute-start | bytes 15560 | tf_op jit(solution)/shard_map/ppermute | solution.py:22
  567.5 4.6 copy-start.20
  577.9 1.2 copy-start.3
  577.9 1.4 copy-start.4
  577.9 1.4 copy-start.22
  577.9 1.4 copy-start.25
  577.9 1.4 copy-start.27
  777.9 353.5 %copy-start.16 = (s32[2048]{0:T(1024)S(1)}, s32[2048]{0:T(1024)}, u32[]{:S(2)}) copy-start(s32[2048]{0:T(1024)} %copy-done.15) | copy-start | bytes 24580
  777.9 365.1 %copy-start.33 = (f32[1,32,64]{2,1,0:T(8,128)S(1)}, f32[1,32,64]{2,1,0:T(8,128)}, u32[]{:S(2)}) copy-start(f32[1,32,64]{2,1,0:T(8,128)} %param.8) | copy-start | bytes 24580
  777.9 371.1 %copy-start.6 = (f32[4,16,16,128]{3,2,1,0:T(8,128)S(1)}, f32[4,16,16,128]{3,2,1,0:T(8,128)}, u32[]{:S(2)}) copy-start(f32[4,16,16,128]{3,2,1,0:T(8,128)} %get-tuple-element.14) | copy-start | bytes 1572868
  1143.8 25.6 %all-to-all-start.2 = ((f32[32,1,256]{2,1,0:T(1,128)}), f32[32,1,256]{2,1,0:T(1,128)S(1)}, u32[]{:S(2)}, u32[]{:S(2)}) async-start(f32[32,1,256]{2,1,0:T(1,128)} %reshape.193), calls=%async_computation.3 | async-start | bytes 65536 | tf_op jit(solution)/shard_map/all_to_all | solution.py:62
  1149.1 8.7 copy-start.18
  1171.1 13.1 all-to-all-start.3
  1176.9 200.8 %reduce-scatter.5.cloned.1.call-start = ((), (), s32[]{:S(2)}) async-start(), calls=%async_computation.7 | async-start | bytes 17825792 | tf_op jit(solution)/shard_map/reduce_scatter | solution.py:75
Sparse Core Ops, SparseCore 0:
  567.6 181.6 reduce-scatter.2
  1204.0 173.6 reduce-scatter.4
where the time goes:
time: 1420 us; the launch traced here: 1410 us
  blocking collectives  770 us (54%)
  waiting for transfers between devices  316 us (22%)
  local copies, waits for them, and re-layouts  151 us (11%)
  other arithmetic  107 us (8%)
  starting transfers between devices  55.2 us (4%)
  between operations  15.2 us (1%)
    all_gather x2, blocking collectives, on_device(): all_nodes = lax.all_gather(shell_disp, ('gy', 'gz'), axis=1, tiled=True)  713 us
    reduce_scatter x2, waiting for transfers between devices, on_device(): lax.psum_scatter(node_terms, ('gy', 'gz'), scatter_dimension=1, tiled=True)  309 us
    psum x2, blocking collectives, on_device(): node_loads = lax.psum(partial_loads, 'gx')  56.9 us
    scatter-add x2, other arithmetic, on_device(): forcing = jnp.zeros_like(flat_vel).at[:, cells_local].add(traction)  40.2 us
    scatter-add x2, other arithmetic, on_device(): jnp.zeros((3, all_nodes.shape[1]), jnp.float32).at[:, elements]  37 us
  transfers between devices with their start and end apart: 18, of which 3 were waited for; matrix products, arithmetic and copies ran while one was open for 9% of the time, Pallas kernels for 0%

commit v1 on v0

--- a/solution.py
+++ b/solution.py
@@ -1,3 +1,4 @@
+import functools
 import jax
 import jax.numpy as jnp
 from jax import lax
@@ -7,6 +8,23 @@
 advection = 0.2
 penalty = 0.5
 relaxation = 0.05
+
+
+def masks_attach(inputs, axis_key):
+    world_n = lax.axis_size(axis_key)
+    rows = [inputs]
+    idx = 1
+    while idx < world_n:
+        v1 = lax.ppermute(rows[idx - 1], axis_key, [(h, (h - 1) % world_n) for h in range(world_n)])
+        rows.append(v1)
+        idx += 1
+    carry_out = jnp.concatenate(rows, axis=1)
+    carry_in = lax.axis_index(axis_key)
+    frame_out = jnp.roll(carry_out, carry_in * inputs.shape[1], axis=1)
+    return frame_out
+
+
+mark_threads = functools.partial(masks_attach, axis_key=("gy", "gz"))
 
 
 def with_halo(cells, sides, width):
@@ -56,7 +74,7 @@
     for iteration in range(ITERS):
         padded = with_halo(fluid_state, (("gx", 1), ("gy", 2), ("gz", 3)), 1)
         halfway = sweep_fluid(padded)
-        all_nodes = lax.all_gather(shell_disp, ("gy", "gz"), axis=1, tiled=True)
+        all_nodes = mark_threads(shell_disp)
         shell_vel = all_nodes[:, elements]
         records = jnp.concatenate([shell_vel, quad_weights[0][None]], 0)
         received = lax.all_to_all(

time: 1420 us -> 890 us (0.63)
  blocking collectives: 770 us -> 56.9 us
  starting transfers between devices: 55.2 us -> 170 us
  waiting for transfers between devices: 316 us -> 363 us
    all_gather x2 -> x0, blocking collectives: 713 us -> none  [on_device(): all_nodes = lax.all_gather(shell_disp, ('gy', 'gz'), axis=1, tiled=True)]
    ppermute x0 -> x30, starting transfers between devices: none -> 119 us  [masks_attach(): lax.ppermute(rows[idx - 1], axis_key, [(h, (h - 1) % world_n) for h in ra...]
    ppermute x0 -> x30, waiting for transfers between devices: none -> 42.5 us  [masks_attach(): lax.ppermute(rows[idx - 1], axis_key, [(h, (h - 1) % world_n) for h in ra...]
    unnamed x92 -> x98, local copies, waits for them, and re-layouts: 14.3 us -> 36.4 us
  transfers between devices with their start and end apart: 18 -> 48, of which waited for: 3 -> 29; matrix products, arithmetic and copies ran while one was open for 9% -> 18% of each run, Pallas kernels for 0% -> 0%
where the time goes in v1:
time: 890 us; the launch traced here: 880 us
  waiting for transfers between devices  363 us (41%)
  starting transfers between devices  170 us (19%)
  local copies, waits for them, and re-layouts  164 us (18%)
  other arithmetic  111 us (12%)
  blocking collectives  56.9 us (6%)
  between operations  15.2 us (2%)
    reduce_scatter x2, waiting for transfers between devices, on_device(): lax.psum_scatter(node_terms, ('gy', 'gz'), scatter_dimension=1, tiled=True)  313 us
    ppermute x30, starting transfers between devices, masks_attach(): lax.ppermute(rows[idx - 1], axis_key, [(h, (h - 1) % world_n) for h in ra...  119 us
    psum x2, blocking collectives, on_device(): node_loads = lax.psum(partial_loads, 'gx')  56.9 us
    ppermute x30, waiting for transfers between devices, masks_attach(): lax.ppermute(rows[idx - 1], axis_key, [(h, (h - 1) % world_n) for h in ra...  42.5 us
    scatter-add x2, other arithmetic, on_device(): forcing = jnp.zeros_like(flat_vel).at[:, cells_local].add(traction)  39.9 us
    scatter-add x2, other arithmetic, on_device(): jnp.zeros((3, all_nodes.shape[1]), jnp.float32).at[:, elements]  36.8 us
    unnamed x98, local copies, waits for them, and re-layouts  36.4 us
    gather x4, local copies, waits for them, and re-layouts, on_device(): shell_vel = all_nodes[:, elements]  24.2 us
  transfers between devices with their start and end apart: 48, of which 29 were waited for; matrix products, arithmetic and copies ran while one was open for 18% of the time, Pallas kernels for 0%

profile of v1, /device:TPU:0, one launch (start us, length us, event | category | flops | bytes accessed | tf_op | source)
XLA Modules:
  0.0 880.2 jit_solution(3950208234733368805)
XLA Ops:
  8.0 4.9 collective-permute-start
  14.1 3.7 collective-permute-start.6
  28.0 4.2 copy.153
  38.4 4.2 copy.152
  42.7 4.4 copy.154
  47.0 8.1 pad_maximum_fusion
  55.2 2.7 copy-done.1
  57.9 4.6 copy.156
  67.0 3.9 collective-permute-start.9
  80.6 3.6 collective-permute-start.11
  85.7 4.4 collective-permute-start.12
  91.8 4.4 collective-permute-start.13
  97.8 4.4 collective-permute-start.14
  103.8 4.4 collective-permute-start.15
  109.9 4.4 collective-permute-start.16
  115.9 4.4 collective-permute-start.17
  122.0 4.4 collective-permute-start.18
  128.0 4.4 collective-permute-start.19
  134.0 4.4 collective-permute-start.20
  141.0 8.5 copy.214
  149.4 11.2 %gather_fusion = f32[2048,3]{1,0:T(8,128)S(1)} fusion(f32[3,32768]{0,1:T(8,128)} %copy.214, s32[2048]{0:T(1024)S(1)} %get-tuple-element.44), kind=kCustom, calls=%fused_computation | custom fusion | bytes 57344 | tf_op jit(solution)/shard_map/gather | solution.py:78
  161.9 7.3 all-to-all-start
  169.3 8.7 copy.168
  178.0 11.2 %gather_fusion.1 = f32[2048,3]{1,0:T(8,128)S(1)} fusion(f32[3,32768]{0,1:T(8,128)} %bitcast.78, s32[2048]{0:T(1024)S(1)} %get-tuple-element.43), kind=kCustom, calls=%fused_computation.1 | custom fusion | bytes 57344 | tf_op jit(solution)/shard_map/gather | solution.py:84
  191.6 18.3 %scatter_custom_fusion = f32[3,32768]{0,1:T(8,128)} fusion(s32[2048]{0:T(1024)S(1)} %reshape.143, f32[2048,3]{1,0:T(8,128)S(1)} %bitcast.86, f32[]{:T(128)} %constant.11.clone.1), kind=kCustom, calls=%fused_computation.14 | custom fusion | flops 6144 | bytes 393220 | tf_op jit(solution)/shard_map/scatter-add | solution.py:86
  209.8 10.0 %copy.172 = f32[3,16,16,128]{3,2,1,0:T(8,128)S(1)} copy(f32[3,16,16,128]{0,3,2,1:T(8,128)} %bitcast.77) | data formatting | bytes 786432 | tf_op jit(solution)/shard_map/reshape | solution.py:87
  219.9 3.8 collective-permute-start.21
  225.8 6.7 all-to-all-start.1
  236.9 4.2 copy.176
  241.9 4.2 copy.175
  246.2 4.3 copy.177
  250.5 8.1 pad_maximum_fusion.1
  258.7 2.7 copy-done
  261.4 3.5 collective-permute-start.25
  266.8 18.4 %scatter_custom_fusion.1 = f32[3,32768]{0,1:T(8,128)} fusion(s32[2048]{0:T(1024)} %copy-done.24, f32[2048,3]{1,0:T(8,128)S(1)} %bitcast.87, f32[]{:T(128)} %constant.11.clone.1), kind=kCustom, calls=%fused_computation.12 | custom fusion | flops 6144 | bytes 393728 | tf_op jit(solution)/shard_map/scatter-add | solution.py:92
  285.2 4.6 copy.179
  295.2 172.5 %reduce-scatter.3.cloned.1.call-done = f32[3,2048]{0,1:T(8,128)} async-done(((f32[3,32768]{0,1:T(8,128)}), f32[3,2048]{0,1:T(8,128)}) %reduce-scatter.3.cloned.1.call-update) | async-done | bytes 24592 | tf_op jit(solution)/shard_map/reduce_scatter | solution.py:93
  467.7 28.4 %psum.14 = f32[3,2048]{0,1:T(8,128)S(1)} all-reduce(f32[3,2048]{0,1:T(8,128)} %reduce-scatter.3.cloned.1.call-done), channel_id=1, replica_groups=mesh['gx'=2,'gy'=4,'gz'=4] {'gx'}, use_global_device_ids=true, to_apply=%region_3.5 | all-reduce | flops 6144 | bytes 49152 | tf_op jit(solution)/shard_map/psum | solution.py:94
  501.7 3.8 collective-permute-start.28
  507.2 4.4 collective-permute-start.29
  513.2 4.4 collective-permute-start.30
  519.2 4.4 collective-permute-start.31
  525.3 4.4 collective-permute-start.32
  531.3 4.4 collective-permute-start.33
  537.5 4.6 collective-permute-start.34
  543.7 4.4 collective-permute-start.35
  549.7 4.4 collective-permute-start.36
  555.8 4.4 collective-permute-start.37
  561.8 4.4 collective-permute-start.38
  567.9 4.4 collective-permute-start.39
  574.1 4.6 collective-permute-start.40
  580.2 4.6 collective-permute-start.41
  587.4 8.5 copy.218
  595.9 12.2 %gather_fusion.2 = f32[2048,3]{1,0:T(8,128)S(1)} fusion(f32[3,32768]{0,1:T(8,128)} %copy.218, s32[2048]{0:T(1024)} %copy-done.11), kind=kCustom, calls=%fused_computation.2 | custom fusion | bytes 57344 | tf_op jit(solution)/shard_map/gather | solution.py:78
  609.9 4.8 all-to-all-start.2
  614.8 8.7 copy.196
  623.5 11.2 %gather_fusion.3 = f32[2048,3]{1,0:T(8,128)S(1)} fusion(f32[3,32768]{0,1:T(8,128)} %bitcast.79, s32[2048]{0:T(1024)S(1)} %copy-done.10), kind=kCustom, calls=%fused_computation.3 | custom fusion | bytes 57344 | tf_op jit(solution)/shard_map/gather | solution.py:84
  636.8 5.8 all-to-all-start.3
  642.7 7.2 all-to-all-done.3
  651.3 18.4 %scatter_custom_fusion.3 = f32[3,32768]{0,1:T(8,128)} fusion(s32[2048]{0:T(1024)} %copy-done.24, f32[2048,3]{1,0:T(8,128)S(1)} %bitcast.85, f32[]{:T(128)} %constant.11.clone.1), kind=kCustom, calls=%fused_computation.8 | custom fusion | flops 6144 | bytes 393728 | tf_op jit(solution)/shard_map/scatter-add | solution.py:92
  670.1 21.6 %scatter_custom_fusion.2 = f32[3,32768]{0,1:T(8,128)} fusion(s32[2048]{0:T(1024)} %copy-done.23, f32[2048,3]{1,0:T(8,128)S(1)} %bitcast.84, f32[]{:T(128)} %constant.11.clone.1), kind=kCustom, calls=%fused_computation.10 | custom fusion | flops 6144 | bytes 393728 | tf_op jit(solution)/shard_map/scatter-add | solution.py:86
  691.7 10.3 %copy.200 = f32[3,16,16,128]{3,2,1,0:T(8,128)S(1)} copy(f32[3,16,16,128]{0,3,2,1:T(8,128)} %bitcast.76) | data formatting | bytes 786432 | tf_op jit(solution)/shard_map/reshape | solution.py:87
  703.0 140.6 %reduce-scatter.5.cloned.1.call-done = f32[3,2048]{0,1:T(8,128)} async-done(((f32[3,32768]{0,1:T(8,128)}), f32[3,2048]{0,1:T(8,128)}) %reduce-scatter.5.cloned.1.call-update) | async-done | bytes 24592 | tf_op jit(solution)/shard_map/reduce_scatter | solution.py:93
  843.5 28.5 %psum.15 = f32[3,2048]{0,1:T(8,128)S(1)} all-reduce(f32[3,2048]{0,1:T(8,128)} %reduce-scatter.5.cloned.1.call-done), channel_id=1, replica_groups=mesh['gx'=2,'gy'=4,'gz'=4] {'gx'}, use_global_device_ids=true, to_apply=%region_7.9 | all-reduce | flops 6144 | bytes 49152 | tf_op jit(solution)/shard_map/psum | solution.py:94
  (232 shorter events, 104.2 us)
Async XLA Ops:
  8.0 18.3 %collective-permute-start = (f32[4,1,16,128]{3,2,1,0:T(8,128)S(1)}, f32[4,1,16,128]{3,2,1,0:T(8,128)S(1)}, u32[]{:S(2)}, u32[]{:S(2)}) collective-permute-start(f32[4,1,16,128]{3,2,1,0:T(8,128)S(1)} %get-tuple-element.37), channel_id=1, source_target_pairs={{0,16},{1,17},{2,18},{3,19},{4,20},{5,21},{6,22},{7,23},{8,24},{9,... | collective-permute-start | bytes 98312 | tf_op jit(solution)/shard_map/ppermute | solution.py:38
  12.8 14.5 %collective-permute-start.1 = (f32[4,1,16,128]{3,2,1,0:T(8,128)S(1)}, f32[4,1,16,128]{3,2,1,0:T(8,128)S(1)}, u32[]{:S(2)}, u32[]{:S(2)}) collective-permute-start(f32[4,1,16,128]{3,2,1,0:T(8,128)S(1)} %get-tuple-element.36), channel_id=1, source_target_pairs={{16,0},{17,1},{18,2},{19,3},{20,4},{21,5},{22,6},{23,7},{24,8},{25... | collective-permute-start | bytes 98312 | tf_op jit(solution)/shard_map/ppermute | solution.py:40
  14.1 11.3 %collective-permute-start.6 = (f32[3,2048]{1,0:T(4,128)}, f32[3,2048]{1,0:T(4,128)S(1)}, u32[]{:S(2)}, u32[]{:S(2)}) collective-permute-start(f32[3,2048]{1,0:T(4,128)} %param.9), channel_id=1, source_target_pairs={{0,15},{1,0},{2,1},{3,2},{4,3},{5,4},{6,5},{7,6},{8,7},{9,8},{10,9... | collective-permute-start | bytes 73736 | tf_op jit(solution)/shard_map/ppermute | solution.py:18
  21.8 20.9 %copy-start.24 = (s32[2048]{0:T(1024)}, s32[2048]{0:T(1024)S(1)}, u32[]{:S(2)}) copy-start(s32[2048]{0:T(1024)S(1)} %reshape.111) | copy-start | bytes 24580
  22.6 169.0 %copy-start.23 = (s32[2048]{0:T(1024)}, s32[2048]{0:T(1024)S(1)}, u32[]{:S(2)}) copy-start(s32[2048]{0:T(1024)S(1)} %reshape.143) | copy-start | bytes 24580
  22.6 126.9 %copy-start.11 = (s32[2048]{0:T(1024)}, s32[2048]{0:T(1024)S(1)}, u32[]{:S(2)}) copy-start(s32[2048]{0:T(1024)S(1)} %get-tuple-element.44) | copy-start | bytes 24580
  22.6 155.4 %copy-start.9 = (s32[2048]{0:T(1024)}, s32[2048]{0:T(1024)S(1)}, u32[]{:S(2)}) copy-start(s32[2048]{0:T(1024)S(1)} %get-tuple-element.43) | copy-start | bytes 24580
  25.4 10.3 %collective-permute-start.7 = (f32[3,2048]{1,0:T(4,128)S(1)}, f32[3,2048]{1,0:T(4,128)S(1)}, u32[]{:S(2)}, u32[]{:S(2)}) collective-permute-start(f32[3,2048]{1,0:T(4,128)S(1)} %collective-permute-done.6), channel_id=1, source_target_pairs={{0,15},{1,0},{2,1},{3,2},{4,3},{5,4},{6,5},{7,6},{8,7},{9,8},{10,9... | collective-permute-start | bytes 73736 | tf_op jit(solution)/shard_map/ppermute | solution.py:18
  28.0 14.7 %copy-start.4 = (f32[4,18,16,128]{3,2,1,0:T(8,128)}, f32[4,18,16,128]{3,2,1,0:T(8,128)S(1)}, u32[]{:S(2)}) copy-start(f32[4,18,16,128]{3,2,1,0:T(8,128)S(1)} %constant_dynamic-update-slice_fusion) | copy-start | bytes 1769476
  32.2 6.2 collective-permute-start.2
  34.4 8.2 collective-permute-start.3
  35.8 31.2 %collective-permute-start.8 = (f32[3,2048]{1,0:T(4,128)S(1)}, f32[3,2048]{1,0:T(4,128)}, u32[]{:S(2)}, u32[]{:S(2)}) collective-permute-start(f32[3,2048]{1,0:T(4,128)S(1)} %collective-permute-done.7), channel_id=1, source_target_pairs={{0,15},{1,0},{2,1},{3,2},{4,3},{5,4},{6,5},{7,6},{8,7},{9,8},{10,9... | collective-permute-start | bytes 73736 | tf_op jit(solution)/shard_map/ppermute | solution.py:18
  55.2 2.7 copy-start.1
  62.4 9.9 %collective-permute-start.4 = (f32[4,18,18,1]{2,1,3,0:T(8,128)S(1)}, f32[4,18,18,1]{2,1,3,0:T(8,128)S(1)}, u32[]{:S(2)}, u32[]{:S(2)}) collective-permute-start(f32[4,18,18,1]{2,1,3,0:T(8,128)S(1)} %get-tuple-element.25), channel_id=1, source_target_pairs={{0,1},{1,2},{2,3},{4,5},{5,6},{6,7},{8,9},{9,10},{10,11},{12,13},{... | collective-permute-start | bytes 15560 | tf_op jit(solution)/shard_map/ppermute | solution.py:38
  64.4 8.5 collective-permute-start.5
  67.0 9.4 %collective-permute-start.9 = (f32[3,2048]{1,0:T(4,128)}, f32[3,2048]{1,0:T(4,128)}, u32[]{:S(2)}, u32[]{:S(2)}) collective-permute-start(f32[3,2048]{1,0:T(4,128)} %collective-permute-done.8), channel_id=1, source_target_pairs={{0,15},{1,0},{2,1},{3,2},{4,3},{5,4},{6,5},{7,6},{8,7},{9,8},{10,9... | collective-permute-start | bytes 73736 | tf_op jit(solution)/shard_map/ppermute | solution.py:18
  74.2 1.2 copy-start.5
  74.2 1.2 copy-start.7
  74.2 1.2 copy-start.12
  74.5 3.4 copy-start.6
  76.4 4.2 collective-permute-start.10
  80.6 5.2 collective-permute-start.11
  85.7 6.0 collective-permute-start.12
  91.8 6.0 collective-permute-start.13
  97.8 6.0 collective-permute-start.14
  103.8 6.0 collective-permute-start.15
  109.9 6.0 collective-permute-start.16
  115.9 6.0 collective-permute-start.17
  122.0 6.0 collective-permute-start.18
  128.0 6.0 collective-permute-start.19
  134.0 6.0 collective-permute-start.20
  141.0 20.1 %copy-start.22 = (f32[1,32,64]{2,1,0:T(8,128)S(1)}, f32[1,32,64]{2,1,0:T(8,128)}, u32[]{:S(2)}) copy-start(f32[1,32,64]{2,1,0:T(8,128)} %param.10) | copy-start | bytes 24580
  161.9 27.7 %all-to-all-start = ((f32[32,1,256]{2,1,0:T(1,128)}), f32[32,1,256]{2,1,0:T(1,128)S(1)}, u32[]{:S(2)}, u32[]{:S(2)}) async-start(f32[32,1,256]{2,1,0:T(1,128)} %reshape.189), calls=%async_computation | async-start | bytes 65536 | tf_op jit(solution)/shard_map/all_to_all | solution.py:80
  219.9 12.6 %collective-permute-start.21 = (f32[4,1,16,128]{3,2,1,0:T(8,128)S(1)}, f32[4,1,16,128]{3,2,1,0:T(8,128)S(1)}, u32[]{:S(2)}, u32[]{:S(2)}) collective-permute-start(f32[4,1,16,128]{3,2,1,0:T(8,128)S(1)} %get-tuple-element.31), channel_id=1, source_target_pairs={{0,16},{1,17},{2,18},{3,19},{4,20},{5,21},{6,22},{7,23},{8,24},{9,... | collective-permute-start | bytes 98312 | tf_op jit(solution)/shard_map/ppermute | solution.py:38
  223.7 8.8 %collective-permute-start.22 = (f32[4,1,16,128]{3,2,1,0:T(8,128)S(1)}, f32[4,1,16,128]{3,2,1,0:T(8,128)S(1)}, u32[]{:S(2)}, u32[]{:S(2)}) collective-permute-start(f32[4,1,16,128]{3,2,1,0:T(8,128)S(1)} %get-tuple-element.32), channel_id=1, source_target_pairs={{16,0},{17,1},{18,2},{19,3},{20,4},{21,5},{22,6},{23,7},{24,8},{25... | collective-permute-start | bytes 98312 | tf_op jit(solution)/shard_map/ppermute | solution.py:40
  225.8 15.3 %all-to-all-start.1 = ((f32[32,1,192]{2,1,0:T(1,128)}), f32[32,1,192]{2,1,0:T(1,128)S(1)}, u32[]{:S(2)}, u32[]{:S(2)}) async-start(f32[32,1,192]{2,1,0:T(1,128)} %reshape.191), calls=%async_computation.1 | async-start | bytes 65536 | tf_op jit(solution)/shard_map/all_to_all | solution.py:89
  232.5 235.2 %reduce-scatter.3.cloned.1.call-start = ((), (), s32[]{:S(2)}) async-start(), calls=%async_computation.6 | async-start | bytes 17825792 | tf_op jit(solution)/shard_map/reduce_scatter | solution.py:93
  232.5 2.3 copy-start.14
  232.6 2.3 copy-start.16
  232.7 9.2 %collective-permute-start.23 = (f32[4,18,1,128]{3,1,2,0:T(8,128)S(1)}, f32[4,18,1,128]{3,1,2,0:T(8,128)S(1)}, u32[]{:S(2)}, u32[]{:S(2)}) collective-permute-start(f32[4,18,1,128]{3,1,2,0:T(8,128)S(1)} %copy.216), channel_id=1, source_target_pairs={{0,4},{4,8},{8,12},{1,5},{5,9},{9,13},{2,6},{6,10},{10,14},{3,7},{... | collective-permute-start | bytes 110600 | tf_op jit(solution)/shard_map/ppermute | solution.py:38
  234.9 11.3 %collective-permute-start.24 = (f32[4,18,1,128]{3,1,2,0:T(8,128)S(1)}, f32[4,18,1,128]{3,1,2,0:T(8,128)S(1)}, u32[]{:S(2)}, u32[]{:S(2)}) collective-permute-start(f32[4,18,1,128]{3,1,2,0:T(8,128)S(1)} %copy.217), channel_id=1, source_target_pairs={{4,0},{8,4},{12,8},{5,1},{9,5},{13,9},{6,2},{10,6},{14,10},{7,3},{... | collective-permute-start | bytes 110600 | tf_op jit(solution)/shard_map/ppermute | solution.py:40
  258.7 2.7 copy-start
  261.4 28.5 %collective-permute-start.25 = (f32[4,18,18,1]{2,1,3,0:T(8,128)S(1)}, f32[4,18,18,1]{2,1,3,0:T(8,128)S(1)}, u32[]{:S(2)}, u32[]{:S(2)}) collective-permute-start(f32[4,18,18,1]{2,1,3,0:T(8,128)S(1)} %get-tuple-element.23), channel_id=1, source_target_pairs={{0,1},{1,2},{2,3},{4,5},{5,6},{6,7},{8,9},{9,10},{10,11},{12,13},{... | collective-permute-start | bytes 15560 | tf_op jit(solution)/shard_map/ppermute | solution.py:38
  264.9 25.6 %collective-permute-start.26 = (f32[4,18,18,1]{2,1,3,0:T(8,128)S(1)}, f32[4,18,18,1]{2,1,3,0:T(8,128)}, u32[]{:S(2)}, u32[]{:S(2)}) collective-permute-start(f32[4,18,18,1]{2,1,3,0:T(8,128)S(1)} %get-tuple-element.24), channel_id=1, source_target_pairs={{1,0},{2,1},{3,2},{5,4},{6,5},{7,6},{9,8},{10,9},{11,10},{13,12},{... | collective-permute-start | bytes 15560 | tf_op jit(solution)/shard_map/ppermute | solution.py:40
  497.8 3.9 collective-permute-start.27
  501.7 5.4 collective-permute-start.28
  507.2 6.0 collective-permute-start.29
  513.2 6.0 collective-permute-start.30
  519.2 6.0 collective-permute-start.31
  525.3 6.0 collective-permute-start.32
  531.3 6.2 collective-permute-start.33
  537.5 6.2 collective-permute-start.34
  543.7 6.0 collective-permute-start.35
  549.7 6.0 collective-permute-start.36
  555.8 6.0 collective-permute-start.37
  561.8 6.0 collective-permute-start.38
  567.9 6.2 collective-permute-start.39
  574.1 6.2 collective-permute-start.40
  580.2 6.2 collective-permute-start.41
  587.4 27.4 %copy-start.3 = (f32[4,16,16,128]{3,2,1,0:T(8,128)S(1)}, f32[4,16,16,128]{3,2,1,0:T(8,128)}, u32[]{:S(2)}) copy-start(f32[4,16,16,128]{3,2,1,0:T(8,128)} %get-tuple-element.15) | copy-start | bytes 1572868
  609.9 25.2 %all-to-all-start.2 = ((f32[32,1,256]{2,1,0:T(1,128)}), f32[32,1,256]{2,1,0:T(1,128)S(1)}, u32[]{:S(2)}, u32[]{:S(2)}) async-start(f32[32,1,256]{2,1,0:T(1,128)} %reshape.193), calls=%async_computation.3 | async-start | bytes 65536 | tf_op jit(solution)/shard_map/all_to_all | solution.py:80
  614.8 8.7 copy-start.10
  636.8 13.1 %all-to-all-start.3 = ((f32[32,1,192]{2,1,0:T(1,128)}), f32[32,1,192]{2,1,0:T(1,128)S(1)}, u32[]{:S(2)}, u32[]{:S(2)}) async-start(f32[32,1,192]{2,1,0:T(1,128)} %reshape.195), calls=%async_computation.4 | async-start | bytes 65536 | tf_op jit(solution)/shard_map/all_to_all | solution.py:89
  642.7 200.9 %reduce-scatter.5.cloned.1.call-start = ((), (), s32[]{:S(2)}) async-start(), calls=%async_computation.7 | async-start | bytes 17825792 | tf_op jit(solution)/shard_map/reduce_scatter | solution.py:93
  (9 other events, 9.1 us)
Sparse Core Ops, SparseCore 0:
  285.4 182.2 reduce-scatter.2
  669.8 173.6 reduce-scatter.4
